TPU v7x, 128 devices: a whole 4x4x4 slice. The times are simulated.
128 devices in a mesh: seq: 16 (over y, z), rep: 8 (over x, core).
Axes of the slice: x: 4, y: 4, z: 4, core: 2. Of those that a mesh axis runs over, the one named last changes fastest.
Arguments:
- mixed: bfloat16 [8, 16, 512, 2048], P('rep', None, None, 'seq'), may hold values from -6 to 6
- decay_in: bfloat16 [8, 16, 2, 2048], P('rep', None, None, 'seq'), may hold values from -6 to 26.6
- beta_in: bfloat16 [8, 16, 2, 2048], P('rep', None, None, 'seq'), may hold values from -6 to 6
- gate_z: bfloat16 [8, 16, 256, 2048], P('rep', None, None, 'seq'), may hold values from -6 to 6
- conv_weight: bfloat16 [4, 16, 512], P(None, 'seq'), may hold values from -3 to 3
- a_log: float32 [32], P('seq'), may hold values from -10 to 3
- dt_bias: float32 [32], P('seq'), may hold values from -5.5 to -3.5
- norm_gain: float32 [128], replicated, may hold values from 0.5 to 1.5
- req_blocks: int32 [8, 8], P('rep'), may hold values from 1 to 8, 32 in all within a row
- replica_of: int32 [8, 8], P('rep'), may hold values from 0 to 7, as said below
- finished: int32 [8, 8], P('rep'), may hold values from 0 to 1
Outputs:
- mixer_out: bfloat16 [8, 16, 256, 2048], P('rep', None, None, 'seq')
- states_out: float32 [8, 16, 32, 128, 128], P('rep', None, 'seq')
- tails_out: bfloat16 [8, 16, 3, 16, 512], P('rep', None, None, 'seq')
Inputs may be any that keep to these rules, and one draw needn't show every extreme that they name: `req_blocks`: blocks of 64 tokens of each of the 8 requests of a pack; together they fill the pack. `replica_of`: at most 2 finished requests of one pack, and at most 16 finished requests of all packs together, name the same replica.
All inputs are finite; a program needn't handle non-finite values.
Results may differ from a plain program's by a relative error of at most 0.012.
Values may be sent and summed in bfloat16 or wider, within the bound.
A program may use at most 64 MiB of HBM per device.

v0:
```python
import jax
import jax.numpy as jnp
from jax import lax
from jax.experimental import pallas as pl
from jax.experimental.pallas import tpu as pltpu
from jax.sharding import PartitionSpec as P

f32, bf16 = jnp.float32, jnp.bfloat16
NC, T, SPAN = 16, 128, 64

def dot(a, b):
    return jnp.dot(a, b, preferred_element_type=f32)

def dot_nt(a, b):
    return lax.dot_general(a, b, (((1,), (1,)), ((), ())), preferred_element_type=f32)

def iota(shape, d):
    return lax.broadcasted_iota(jnp.int32, shape, d)

def setup_tables(s):
    j, i = iota((T, T), 0), iota((T, T), 1)
    same = (j // SPAN) == (i // SPAN)
    s.seen[...] = jnp.where(same & (j <= i), 1.0, 0.0)
    s.later[...] = jnp.where(same & (j < i), 1.0, 0.0)
    s.eye[...] = jnp.where(j == i, 1.0, 0.0)
    for level in range(6):
        s.level[level] = jnp.where(((j ^ i) >> level) == 1, 1.0, 0.0).astype(bf16)
    taps = s.conv_weight[...].reshape(4, 512).astype(f32)
    taps = jnp.concatenate([taps, jnp.zeros((4, 512), f32)], axis=0).T
    for tap in range(4):
        s.taps[tap] = jnp.broadcast_to(taps[:, tap:tap + 1], (512, T))
    block = iota((32, T), 0)
    start = jnp.int32(0)
    hit = jnp.zeros((32, T), f32)
    for q in range(8):
        hit = jnp.where(block == start, 1.0, hit)
        start = start + s.req_blocks[0, q]
    s.stay[...] = 1.0 - hit

def setup_gates(s):
    lane = iota((NC, T), 1)
    for r in range(2):
        x = s.aux[:, r, :] + s.dt_bias[r]
        rate = jnp.exp(jnp.full((NC, T), s.a_log[r], f32))
        decay = -rate * (jnp.maximum(x, 0.0) + jnp.log1p(jnp.exp(-jnp.abs(x))))
        c = decay
        for sh in (1, 2, 4, 8, 16, 32):
            c = c + jnp.where(lane % SPAN >= sh, pltpu.roll(c, sh, 1), 0.0)
        end0 = jnp.broadcast_to(c[:, SPAN - 1:SPAN], (NC, T))
        end1 = jnp.broadcast_to(c[:, T - 1:T], (NC, T))
        s.cum[r] = c
        s.fade[r] = jnp.exp(jnp.where(lane < SPAN, end0, end1) - c)
        s.lift[r] = jnp.exp(c)
        s.beta[r] = 1.0 / (1.0 + jnp.exp(-s.aux[:, 2 + r, :]))
        s.keep[r, 0] = jnp.exp(end0)
        s.keep[r, 1] = jnp.exp(end1)

def row(ref, c):
    return ref[pl.ds(c, 1), :]

def prep_chunk(s, c):
    before = lax.rem(c + NC - 1, NC)
    lane = iota((1, T), 1)
    token = lane + c * T
    start = jnp.int32(0)
    since = token
    for q in range(7):
        start = start + s.req_blocks[0, q] * SPAN
        since = jnp.where(token >= start, token - start, since)
    now = s.x[c]
    old = s.x[before]
    parts = []
    for g in range(4):
        rows = slice(g * T, (g + 1) * T)
        cur = now[rows].astype(f32)
        prev = old[rows].astype(f32)
        total = s.taps[3, rows, :] * cur
        for back in (1, 2, 3):
            moved = pltpu.roll(jnp.where(lane >= T - back, prev, cur), back, 1)
            total = total + s.taps[3 - back, rows, :] * jnp.where(since >= back, moved, 0.0)
        parts.append(total / (1.0 + jnp.exp(-total)))
    qT = parts[0].astype(bf16)
    kw = parts[1].astype(bf16).astype(f32)
    kT32 = kw * lax.rsqrt(jnp.sum(kw * kw, axis=0, keepdims=True) + 1e-6)
    kT = kT32.astype(bf16)
    kT32 = kT.astype(f32)
    k = kT32.T.astype(bf16)
    both = dot(k, jnp.concatenate([kT, qT], axis=1))
    gram, raw = both[:, :T], both[:, T:]
    zero = jnp.zeros((SPAN, T), bf16)
    kk = jnp.concatenate([
        jnp.concatenate([k[:SPAN], zero], axis=0),
        jnp.concatenate([zero, k[SPAN:]], axis=0)], axis=1)
    seen, later = s.seen[...], s.later[...]
    minus, scaled = [], []
    for r in range(2):
        cum = row(s.cum.at[r], c)
        col = jnp.broadcast_to(cum, (T, T)).T
        e = jnp.exp((cum - col) * seen) * seen
        s.score[c, r] = (raw * e).astype(bf16)
        n = gram * e * later * row(s.beta.at[r], c)
        minus.append(n)
    low = [n.astype(bf16) for n in minus]
    u = [(s.eye[...] - n * s.level[0].astype(f32)).astype(bf16) for n in minus]
    for level in range(1, 6):
        p = [dot(u[r], low[r] * s.level[level]).astype(bf16) for r in range(2)]
        u = [u[r] - dot(p[r], u[r]).astype(bf16) for r in range(2)]
    for r in range(2):
        rest = (minus[r] - low[r].astype(f32)).astype(bf16)
        nx = dot(jnp.concatenate([low[r], rest], axis=0), u[r])
        res = s.eye[...] - u[r].astype(f32) - (nx[:T] + nx[T:])
        u[r] = (u[r].astype(f32) + dot(u[r], res.astype(bf16))).astype(bf16)
    for r in range(2):
        beta = row(s.beta.at[r], c)
        sk = (kT32 * (beta * row(s.lift.at[r], c))).astype(bf16)
        sv = (parts[2 + r].astype(bf16).astype(f32) * beta).astype(bf16)
        w = dot(jnp.concatenate([sv, sk], axis=0), u[r])
        wb = w.astype(bf16)
        s.wv[c, r] = wb[:T]
        s.wq[c, r, :, :T] = wb[T:]
        s.wq[c, r, :, T:] = qT
        gw = dot((w * row(s.fade.at[r], c)).astype(bf16), kk)
        for b in range(2):
            s.add[c, r, b] = gw[:T, b * T:(b + 1) * T]
            s.turn[c, r, b] = gw[T:, b * T:(b + 1) * T].astype(bf16)
    j, i = iota((16, T), 0), iota((16, T), 1)
    pick = jnp.where((j % 8 < 3) & (i == (j // 8) * SPAN + SPAN - 3 + j % 8), 1.0, 0.0).astype(bf16)
    tails = dot_nt(pick, now)
    s.tails[2 * c] = tails[:8]
    s.tails[2 * c + 1] = tails[8:]

def scan_blocks(s):
    def step(c, carry):
        state = list(carry)
        for b in range(2):
            stay = row(s.stay, 2 * c + b)
            for r in range(2):
                inside = state[r] * stay
                low = inside.astype(bf16)
                s.enter[c, r, b * T:(b + 1) * T, :] = low
                state[r] = (row(s.keep.at[r, b], c) * inside + s.add[c, r, b]) - dot(low, s.turn[c, r, b])
                s.leave[2 * c + b, r] = state[r].astype(bf16)
        return tuple(state)
    zero = jnp.zeros((T, T), f32)
    lax.fori_loop(0, NC, step, (zero, zero))

def post_chunk(s, c):
    lane = iota((1, T), 1)
    for r in range(2):
        both = dot(s.enter[c, r], s.wq[c, r])
        first = lane < SPAN
        seenk = jnp.where(first, both[:T, :T], both[T:, :T])
        seenq = jnp.where(first, both[:T, T:], both[T:, T:])
        new = (s.wv[c, r].astype(f32) - seenk).astype(bf16)
        out = row(s.lift.at[r], c) * seenq + dot(new, s.score[c, r])
        s.core[c, r * T:(r + 1) * T, :] = out.astype(bf16)

SCRATCH = dict(
    x=((NC, 512, T), bf16), aux=((NC, 8, T), f32),
    cum=((2, NC, T), f32), fade=((2, NC, T), f32), lift=((2, NC, T), f32), beta=((2, NC, T), f32),
    keep=((2, 2, NC, T), f32), stay=((32, T), f32),
    seen=((T, T), f32), later=((T, T), f32), eye=((T, T), f32), level=((6, T, T), bf16),
    taps=((4, 512, T), f32),
    wv=((NC, 2, T, T), bf16), wq=((NC, 2, T, 2 * T), bf16), score=((NC, 2, T, T), bf16),
    add=((NC, 2, 2, T, T), f32), turn=((NC, 2, 2, T, T), bf16),
    enter=((NC, 2, 2 * T, T), bf16), leave=((32, 2, T, T), bf16),
    core=((NC, 256, T), bf16), tails=((32, 8, 512), f32),
)

class Refs:
    pass


N_SEQ, N_REP, REQS, CAP = 16, 8, 8, 2
MESH = pl.DeviceIdType.MESH
VMEM = pl.BlockSpec(memory_space=pltpu.VMEM)
SMEM = pl.BlockSpec(memory_space=pltpu.SMEM)
ANY = pl.BlockSpec(memory_space=pl.ANY)
SCRATCH_NAMES = list(SCRATCH)


def fill_slots(s):
    keys, lasts = [], []
    last = jnp.int32(-1)
    for q in range(REQS):
        last = last + s.req_blocks[0, q]
        rank = jnp.int32(0)
        for p in range(q):
            hit = (s.replica_of[0, p] == s.replica_of[0, q]) & (s.finished[0, p] > 0)
            rank = rank + jnp.where(hit, 1, 0)
        keys.append(jnp.where(s.finished[0, q] > 0, s.replica_of[0, q] * CAP + rank, -1))
        lasts.append(last)
    for m in range(N_REP * CAP):
        where, used = jnp.int32(0), jnp.int32(0)
        for q in range(REQS):
            where = where + jnp.where(keys[q] == m, lasts[q], 0)
            used = used + jnp.where(keys[q] == m, 1, 0)
        s.slot_block[m] = where
        s.slot_used[m] = used


def build_slot(s, d, k):
    m = d * CAP + k
    block, used = s.slot_block[m], s.slot_used[m].astype(f32)
    for r in range(2):
        flipped = dot_nt(s.eye[...].astype(bf16), s.leave[block, r])
        s.out_states[d, k, r] = (flipped * used).astype(bf16)
    count = (s.slot_used[d * CAP] + s.slot_used[d * CAP + 1]).astype(f32)
    rows = s.tails[block] * used
    return jnp.where(iota((8, 512), 0) == 3, count, rows)


def main_kernel(mixed, decay_in, beta_in, conv_weight, a_log, dt_bias, req_blocks, replica_of, finished,
                back, got_states, got_tails, *scratch):
    s = Refs()
    names = SCRATCH_NAMES + [
        "aux_out", "out_states", "out_tails", "slot_block", "slot_used",
        "x_send", "x_recv", "aux_send", "aux_recv", "core_send", "core_recv",
        "st_send", "st_recv", "tl_send", "tl_recv", "own"]
    for name, ref in zip(names, scratch):
        setattr(s, name, ref)
    s.conv_weight, s.a_log, s.dt_bias, s.req_blocks = conv_weight, a_log, dt_bias, req_blocks
    s.replica_of, s.finished = replica_of, finished
    me, rep = lax.axis_index("seq"), lax.axis_index("rep")

    barrier = pltpu.get_barrier_semaphore()
    for k in range(1, N_SEQ):
        pl.semaphore_signal(barrier, inc=1, device_id={"seq": lax.rem(me + k, N_SEQ)}, device_id_type=MESH)
    for k in range(1, N_REP):
        pl.semaphore_signal(barrier, inc=1, device_id={"rep": lax.rem(rep + k, N_REP)}, device_id_type=MESH)
    for h in range(N_SEQ):
        s.aux_out[h, 0:2, :] = decay_in[0, h].astype(f32)
        s.aux_out[h, 2:4, :] = beta_in[0, h].astype(f32)
        s.aux_out[h, 4:8, :] = jnp.zeros((4, T), f32)

    own_x = pltpu.make_async_copy(mixed.at[0, me], s.x.at[me], s.own.at[0])
    own_aux = pltpu.make_async_copy(s.aux_out.at[me], s.aux.at[me], s.own.at[1])
    own_x.start()
    own_aux.start()
    pl.semaphore_wait(barrier, N_SEQ + N_REP - 2)

    def aux_copy(k):
        to = lax.rem(me + N_SEQ - k, N_SEQ)
        return pltpu.make_async_remote_copy(
            src_ref=s.aux_out.at[to], dst_ref=s.aux.at[me], send_sem=s.aux_send.at[k], recv_sem=s.aux_recv.at[k],
            device_id={"seq": to}, device_id_type=MESH)

    def x_copy(k):
        to = lax.rem(me + N_SEQ - k, N_SEQ)
        return pltpu.make_async_remote_copy(
            src_ref=mixed.at[0, to], dst_ref=s.x.at[me], send_sem=s.x_send.at[k], recv_sem=s.x_recv.at[k],
            device_id={"seq": to}, device_id_type=MESH)

    def start_inputs(k, carry):
        aux_copy(k).start()
        x_copy(k).start()
        return carry

    lax.fori_loop(1, N_SEQ, start_inputs, 0)
    setup_tables(s)
    fill_slots(s)
    own_x.wait()
    own_aux.wait()

    def wait_aux(k, carry):
        aux_copy(k).wait_recv()
        return carry

    lax.fori_loop(1, N_SEQ, wait_aux, 0)
    setup_gates(s)

    def prep(k, carry):
        @pl.when(k < N_SEQ)
        def _():
            x_copy(k).wait_recv()

        prep_chunk(s, lax.rem(me + k, N_SEQ))
        return carry

    lax.fori_loop(1, N_SEQ + 1, prep, 0)
    scan_blocks(s)

    def core_copy(k):
        to = lax.rem(me + k, N_SEQ)
        return pltpu.make_async_remote_copy(
            src_ref=s.core.at[to], dst_ref=back.at[me], send_sem=s.core_send.at[k], recv_sem=s.core_recv.at[k],
            device_id={"seq": to}, device_id_type=MESH)

    def state_copies(k):
        to = lax.rem(rep + k, N_REP)
        return [
            pltpu.make_async_remote_copy(
                src_ref=s.out_states.at[to], dst_ref=got_states.at[rep], send_sem=s.st_send.at[k],
                recv_sem=s.st_recv.at[k], device_id={"rep": to}, device_id_type=MESH),
            pltpu.make_async_remote_copy(
                src_ref=s.out_tails.at[to], dst_ref=got_tails.at[rep], send_sem=s.tl_send.at[k],
                recv_sem=s.tl_recv.at[k], device_id={"rep": to}, device_id_type=MESH)]

    def post(k, carry):
        for half in range(2):
            j = 2 * k - 1 + half
            post_chunk(s, lax.rem(me + j, N_SEQ))

            @pl.when(j < N_SEQ)
            def _():
                core_copy(j).start()

        d = lax.rem(rep + k, N_REP)
        tails = [build_slot(s, d, slot) for slot in range(CAP)]
        s.out_tails[d] = jnp.concatenate(tails, axis=0).astype(bf16)

        @pl.when(k < N_REP)
        def _():
            for copy in state_copies(k):
                copy.start()

        return carry

    lax.fori_loop(1, N_REP + 1, post, 0)
    own = [
        pltpu.make_async_copy(s.core.at[me], back.at[me], s.own.at[2]),
        pltpu.make_async_copy(s.out_states.at[rep], got_states.at[rep], s.own.at[3]),
        pltpu.make_async_copy(s.out_tails.at[rep], got_tails.at[rep], s.own.at[4])]
    for copy in own:
        copy.start()

    def finish_seq(k, carry):
        aux_copy(k).wait_send()
        x_copy(k).wait_send()
        core_copy(k).wait()
        return carry

    def finish_rep(k, carry):
        for copy in state_copies(k):
            copy.wait()
        return carry

    lax.fori_loop(1, N_SEQ, finish_seq, 0)
    lax.fori_loop(1, N_REP, finish_rep, 0)
    for copy in own:
        copy.wait()


HEADS = 4


def finish_kernel(back, gate, gain, got_states, got_tails, mixer, states, tails):
    step = pl.program_id(0)
    column = jnp.broadcast_to(gain[...], (T, T)).T
    for h in range(HEADS):
        for r in range(2):
            rows = slice(r * T, (r + 1) * T)
            value = back[h, rows, :].astype(f32)
            inverse = lax.rsqrt(jnp.mean(value * value, axis=0, keepdims=True) + 1e-6)
            z = gate[0, h, rows, :].astype(f32)
            mixer[0, h, rows, :] = (value * inverse * column * (z / (1.0 + jnp.exp(-z)))).astype(bf16)
    counts = [jnp.max(got_tails[q, 0:8, 0:T].astype(f32)[3:4]).astype(jnp.int32) for q in range(N_REP)]
    bases, base = [], jnp.int32(0)
    for q in range(N_REP):
        bases.append(base)
        base = base + counts[q]
    for h in range(HEADS):
        slot = step * HEADS + h
        pick, used = jnp.int32(0), jnp.int32(0)
        for q in range(N_REP):
            for k in range(CAP):
                hit = (bases[q] + k == slot) & (counts[q] > k)
                pick = pick + jnp.where(hit, q * CAP + k, 0)
                used = used + jnp.where(hit, 1, 0)
        scale = used.astype(f32)
        source, rank = pick // CAP, pick % CAP
        for r in range(2):
            states[0, h, r] = got_states[source, rank, r].astype(f32) * scale
        both = got_tails[source].astype(f32)
        rows = jnp.where(rank == 0, both[0:8], both[8:16]) * scale
        tails[0, h, :, 0, :] = rows[0:3].astype(bf16)


def body(mixed, decay_in, beta_in, gate_z, conv_weight, a_log, dt_bias, norm_gain, req_blocks, replica_of, finished):
    dma = pltpu.SemaphoreType.DMA
    back, got_states, got_tails = pl.pallas_call(
        main_kernel,
        name="main",
        out_shape=[
            jax.ShapeDtypeStruct((N_SEQ, 2 * T, T), bf16),
            jax.ShapeDtypeStruct((N_REP, CAP, 2, T, T), bf16),
            jax.ShapeDtypeStruct((N_REP, 16, 512), bf16)],
        in_specs=[ANY, VMEM, VMEM, VMEM] + [SMEM] * 5,
        out_specs=[ANY] * 3,
        scratch_shapes=[pltpu.VMEM(*SCRATCH[name]) for name in SCRATCH_NAMES] + [
            pltpu.VMEM((N_SEQ, 8, T), f32),
            pltpu.VMEM((N_REP, CAP, 2, T, T), bf16),
            pltpu.VMEM((N_REP, 16, 512), bf16),
            pltpu.SMEM((N_REP * CAP,), jnp.int32),
            pltpu.SMEM((N_REP * CAP,), jnp.int32)] + [dma((N_SEQ,))] * 6 + [dma((N_REP,))] * 4 + [dma((5,))],
        compiler_params=pltpu.CompilerParams(
            collective_id=0, has_side_effects=True, vmem_limit_bytes=48 << 20),
    )(mixed, decay_in, beta_in, conv_weight, a_log, dt_bias, req_blocks, replica_of, finished)
    whole = lambda shape: pl.BlockSpec(shape, lambda i: (0,) * len(shape))
    mixer, states, tails = pl.pallas_call(
        finish_kernel,
        name="finish",
        grid=(N_SEQ // HEADS,),
        out_shape=[
            jax.ShapeDtypeStruct((1, N_SEQ, 2 * T, T), bf16),
            jax.ShapeDtypeStruct((1, N_REP * CAP, 2, T, T), f32),
            jax.ShapeDtypeStruct((1, N_REP * CAP, 3, 1, 512), bf16)],
        in_specs=[
            pl.BlockSpec((HEADS, 2 * T, T), lambda i: (i, 0, 0)),
            pl.BlockSpec((1, HEADS, 2 * T, T), lambda i: (0, i, 0, 0)),
            whole((1, T)),
            whole((N_REP, CAP, 2, T, T)),
            whole((N_REP, 16, 512))],
        out_specs=[
            pl.BlockSpec((1, HEADS, 2 * T, T), lambda i: (0, i, 0, 0)),
            pl.BlockSpec((1, HEADS, 2, T, T), lambda i: (0, i, 0, 0, 0)),
            pl.BlockSpec((1, HEADS, 3, 1, 512), lambda i: (0, i, 0, 0, 0))],
    )(back, gate_z, norm_gain.reshape(1, T), got_states, got_tails)
    return mixer, states, tails


def solution(mesh):
    placed = P("rep", None, None, "seq")
    return jax.shard_map(
        body,
        mesh=mesh,
        in_specs=(placed, placed, placed, placed, P(None, "seq", None), P("seq"), P("seq"), P(),
                  P("rep", None), P("rep", None), P("rep", None)),
        out_specs=(placed, P("rep", None, "seq", None, None), P("rep", None, None, "seq", None)),
        check_vma=False,
    )
```

profile of v0, /device:TPU:11, one launch (start us, length us, event | category | flops | bytes accessed | tf_op | source)
XLA Modules:
  0.0 122.8 jit_solution(4786946303752105271)
XLA Ops:
  0.6 0.7 copy.14.conv_weight
  1.3 0.0 copy-start
  1.3 1.6 %copy-done = bf16[1,16,512,128]{3,2,1,0:T(8,128)(2,1)S(1)} copy-done((bf16[1,16,512,128]{3,2,1,0:T(8,128)(2,1)S(1)}, bf16[1,16,512,128]{3,2,1,0:T(8,128)(2,1)}, u32[]{:S(2)}) %copy-start) | copy-done | bytes 2097176
  2.9 0.0 copy-start.4
  2.9 0.7 copy-done.4
  3.6 0.0 copy-start.5
  3.6 0.7 copy-done.5
  4.3 0.0 copy-start.6
  4.3 0.7 copy-done.6
  5.0 0.0 copy-start.7
  5.0 0.7 copy-done.7
  5.6 0.0 copy-start.8
  5.6 0.7 copy-done.8
  6.3 0.0 copy-start.9
  6.3 0.7 copy-done.9
  6.9 0.0 copy-start.10
  6.9 0.7 copy-done.10
  7.6 106.1 %main.1 = (bf16[16,256,128]{2,1,0:T(8,128)(2,1)S(1)}, bf16[8,2,2,128,128]{4,3,2,1,0:T(8,128)(2,1)S(1)}, bf16[8,16,512]{2,1,0:T(8,128)(2,1)S(1)}) custom-call(bf16[1,16,512,128]{3,2,1,0:T(8,128)(2,1)S(1)} %copy-done, bf16[1,16,2,128]{3,2,1,0:T(2,128)(2,1)S(1)} %copy-done.4, bf16[1,16,2,128]{3,2,1,0:T(2,128)(2,1)S(1)} %copy-done.5, ...), custom_call_target="tpu_custom_call" | custom-call | tf_op jit(solution)/shard_map/main/pallas_call | solution.py:381
  113.7 0.0 copy-start.1
  113.7 1.0 copy-done.1
  114.7 0.0 copy-start.2
  114.7 1.0 copy-done.2
  115.7 0.0 copy-start.3
  115.7 0.6 copy-done.3
  116.4 4.9 %finish.1 = (bf16[1,16,256,128]{3,2,1,0:T(8,128)(2,1)}, f32[1,16,2,128,128]{4,3,2,1,0:T(8,128)}, bf16[1,16,3,1,512]{4,3,2,1,0:T(2,128)(2,1)}) custom-call(bf16[16,256,128]{2,1,0:T(8,128)(2,1)} %copy-done.1, bf16[1,16,256,128]{3,2,1,0:T(8,128)(2,1)} %gate.1, f32[1,128]{1,0:T(1,128)} %bitcast.1, bf16[8,2,2,128,128]{4,3,2,1,0:T(8,128)(2,1)} %copy-done.2, ...), custom_call_target="tpu_custom_call" | custom-call | tf_op jit(solution)/shard_map/finish/pallas_call | solution.py:400
  121.3 1.5 %copy.15 = bf16[1,16,3,1,512]{4,1,3,2,0:T(8,128)(2,1)} copy(bf16[1,16,3,1,512]{4,3,2,1,0:T(2,128)(2,1)} %get-tuple-element.11) | data formatting | bytes 98304 | tf_op jit(solution)/shard_map/finish/pallas_call | solution.py:400
Async XLA Ops:
  1.3 1.6 %copy-start = (bf16[1,16,512,128]{3,2,1,0:T(8,128)(2,1)S(1)}, bf16[1,16,512,128]{3,2,1,0:T(8,128)(2,1)}, u32[]{:S(2)}) copy-start(bf16[1,16,512,128]{3,2,1,0:T(8,128)(2,1)} %mixed.1) | copy-start | bytes 6291460
  2.9 0.7 copy-start.4
  3.6 0.7 copy-start.5
  4.3 0.7 copy-start.6
  5.0 0.7 copy-start.7
  5.6 0.7 copy-start.8
  6.3 0.7 copy-start.9
  6.9 0.7 copy-start.10
  113.7 1.0 copy-start.1
  114.7 1.0 copy-start.2
  115.7 0.6 copy-start.3
where the time goes:
time: 123 us
  Pallas kernels  111 us (90%)
  local copies, waits for them, and re-layouts  11.1 us (9%)
    pallas_call x1, Pallas kernels, body(): pl.pallas_call(main_kernel, name='main', out_shape=[jax.ShapeDtypeStruct(...  106 us
    unnamed x23, local copies, waits for them, and re-layouts  9.56 us
    pallas_call x1, Pallas kernels, body(): pl.pallas_call(finish_kernel, name='finish', grid=(N_SEQ // HEADS,), out_...  4.89 us

commit v1 on v0

--- a/solution.py
+++ b/solution.py
@@ -58,7 +58,7 @@
 def row(ref, c):
     return ref[pl.ds(c, 1), :]
 
-def prep_chunk(s, c):
+def read_chunk(s, c):
     before = lax.rem(c + NC - 1, NC)
     lane = iota((1, T), 1)
     token = lane + c * T
@@ -78,42 +78,51 @@
         for back in (1, 2, 3):
             moved = pltpu.roll(jnp.where(lane >= T - back, prev, cur), back, 1)
             total = total + s.taps[3 - back, rows, :] * jnp.where(since >= back, moved, 0.0)
-        parts.append(total / (1.0 + jnp.exp(-total)))
-    qT = parts[0].astype(bf16)
-    kw = parts[1].astype(bf16).astype(f32)
-    kT32 = kw * lax.rsqrt(jnp.sum(kw * kw, axis=0, keepdims=True) + 1e-6)
-    kT = kT32.astype(bf16)
-    kT32 = kT.astype(f32)
-    k = kT32.T.astype(bf16)
+        parts.append((total / (1.0 + jnp.exp(-total))).astype(bf16))
+    qT = parts[0]
+    kw = parts[1].astype(f32)
+    kT = (kw * lax.rsqrt(jnp.sum(kw * kw, axis=0, keepdims=True) + 1e-6)).astype(bf16)
+    k = kT.astype(f32).T.astype(bf16)
     both = dot(k, jnp.concatenate([kT, qT], axis=1))
     gram, raw = both[:, :T], both[:, T:]
+    minus = []
+    for r in range(2):
+        cum = row(s.cum.at[r], c)
+        col = jnp.broadcast_to(cum, (T, T)).T
+        e = jnp.exp((cum - col) * s.seen[...]) * s.seen[...]
+        s.score[c, r] = (raw * e).astype(bf16)
+        minus.append(gram * e * (s.later[...] * row(s.beta.at[r], c)))
+    j, i = iota((16, T), 0), iota((16, T), 1)
+    pick = jnp.where((j % 8 < 3) & (i == (j // 8) * SPAN + SPAN - 3 + j % 8), 1.0, 0.0).astype(bf16)
+    tails = dot_nt(pick, now)
+    s.tails[2 * c] = tails[:8]
+    s.tails[2 * c + 1] = tails[8:]
+    return qT, kT, k, parts[2:], minus
+
+
+def solve(s, minus):
+    low = [n.astype(bf16) for n in minus]
+    count = range(len(minus))
+    u = [(s.eye[...] - n * s.level[0].astype(f32)).astype(bf16) for n in minus]
+    for level in range(1, 6):
+        p = [dot(u[m], low[m] * s.level[level]).astype(bf16) for m in count]
+        u = [u[m] - dot(p[m], u[m]).astype(bf16) for m in count]
+    rest = [(minus[m] - low[m].astype(f32)).astype(bf16) for m in count]
+    nx = [dot(jnp.concatenate([low[m], rest[m]], axis=0), u[m]) for m in count]
+    res = [(s.eye[...] - u[m].astype(f32) - (nx[m][:T] + nx[m][T:])).astype(bf16) for m in count]
+    return [(u[m].astype(f32) + dot(u[m], res[m])).astype(bf16) for m in count]
+
+
+def weigh(s, c, data, u):
+    qT, kT, k, values, _ = data
     zero = jnp.zeros((SPAN, T), bf16)
     kk = jnp.concatenate([
         jnp.concatenate([k[:SPAN], zero], axis=0),
         jnp.concatenate([zero, k[SPAN:]], axis=0)], axis=1)
-    seen, later = s.seen[...], s.later[...]
-    minus, scaled = [], []
-    for r in range(2):
-        cum = row(s.cum.at[r], c)
-        col = jnp.broadcast_to(cum, (T, T)).T
-        e = jnp.exp((cum - col) * seen) * seen
-        s.score[c, r] = (raw * e).astype(bf16)
-        n = gram * e * later * row(s.beta.at[r], c)
-        minus.append(n)
-    low = [n.astype(bf16) for n in minus]
-    u = [(s.eye[...] - n * s.level[0].astype(f32)).astype(bf16) for n in minus]
-    for level in range(1, 6):
-        p = [dot(u[r], low[r] * s.level[level]).astype(bf16) for r in range(2)]
-        u = [u[r] - dot(p[r], u[r]).astype(bf16) for r in range(2)]
-    for r in range(2):
-        rest = (minus[r] - low[r].astype(f32)).astype(bf16)
-        nx = dot(jnp.concatenate([low[r], rest], axis=0), u[r])
-        res = s.eye[...] - u[r].astype(f32) - (nx[:T] + nx[T:])
-        u[r] = (u[r].astype(f32) + dot(u[r], res.astype(bf16))).astype(bf16)
     for r in range(2):
         beta = row(s.beta.at[r], c)
-        sk = (kT32 * (beta * row(s.lift.at[r], c))).astype(bf16)
-        sv = (parts[2 + r].astype(bf16).astype(f32) * beta).astype(bf16)
+        sk = (kT.astype(f32) * (beta * row(s.lift.at[r], c))).astype(bf16)
+        sv = (values[r].astype(f32) * beta).astype(bf16)
         w = dot(jnp.concatenate([sv, sk], axis=0), u[r])
         wb = w.astype(bf16)
         s.wv[c, r] = wb[:T]
@@ -123,11 +132,14 @@
         for b in range(2):
             s.add[c, r, b] = gw[:T, b * T:(b + 1) * T]
             s.turn[c, r, b] = gw[T:, b * T:(b + 1) * T].astype(bf16)
-    j, i = iota((16, T), 0), iota((16, T), 1)
-    pick = jnp.where((j % 8 < 3) & (i == (j // 8) * SPAN + SPAN - 3 + j % 8), 1.0, 0.0).astype(bf16)
-    tails = dot_nt(pick, now)
-    s.tails[2 * c] = tails[:8]
-    s.tails[2 * c + 1] = tails[8:]
+
+
+def prep_chunks(s, chunks):
+    data = [read_chunk(s, c) for c in chunks]
+    minus = [n for d in data for n in d[4]]
+    u = solve(s, minus)
+    for m, c in enumerate(chunks):
+        weigh(s, c, data[m], u[2 * m:2 * m + 2])
 
 def scan_blocks(s):
     def step(c, carry):
@@ -144,16 +156,17 @@
     zero = jnp.zeros((T, T), f32)
     lax.fori_loop(0, NC, step, (zero, zero))
 
-def post_chunk(s, c):
-    lane = iota((1, T), 1)
-    for r in range(2):
-        both = dot(s.enter[c, r], s.wq[c, r])
-        first = lane < SPAN
-        seenk = jnp.where(first, both[:T, :T], both[T:, :T])
-        seenq = jnp.where(first, both[:T, T:], both[T:, T:])
-        new = (s.wv[c, r].astype(f32) - seenk).astype(bf16)
-        out = row(s.lift.at[r], c) * seenq + dot(new, s.score[c, r])
-        s.core[c, r * T:(r + 1) * T, :] = out.astype(bf16)
+def post_chunks(s, chunks):
+    first = iota((1, T), 1) < SPAN
+    for c in chunks:
+        for r in range(2):
+            both = dot(s.enter[c, r], s.wq[c, r])
+            seenk = jnp.where(first, both[:T, :T], both[T:, :T])
+            seenq = jnp.where(first, both[:T, T:], both[T:, T:])
+            new = (s.wv[c, r].astype(f32) - seenk).astype(bf16)
+            out = row(s.lift.at[r], c) * seenq + dot(new, s.score[c, r])
+            s.core[c, r * T:(r + 1) * T, :] = out.astype(bf16)
+
 
 SCRATCH = dict(
     x=((NC, 512, T), bf16), aux=((NC, 8, T), f32),
@@ -172,6 +185,7 @@
 
 
 N_SEQ, N_REP, REQS, CAP = 16, 8, 8, 2
+AHEAD = 8
 MESH = pl.DeviceIdType.MESH
 VMEM = pl.BlockSpec(memory_space=pltpu.VMEM)
 SMEM = pl.BlockSpec(memory_space=pltpu.SMEM)
@@ -210,17 +224,35 @@
     return jnp.where(iota((8, 512), 0) == 3, count, rows)
 
 
+ORDER = (1, 15, 4, 12, 5, 11, 3, 13, 2, 14, 6, 10, 8, 7, 9)
+GROUPS = ((1, 0, 5, 12), (4, 13, 2, 15), (3, 14, 6, 11), (7, 10, 8, 9))
+READY = (0, 6, 10, 12, 15)
+REP_ORDER = (2, 6, 1, 7, 3, 5, 4, 0)
+
+
+def entry(table, i):
+    out = jnp.int32(table[0])
+    for t in range(1, len(table)):
+        out = jnp.where(i == t, table[t], out)
+    return out
+
+
 def main_kernel(mixed, decay_in, beta_in, conv_weight, a_log, dt_bias, req_blocks, replica_of, finished,
                 back, got_states, got_tails, *scratch):
     s = Refs()
     names = SCRATCH_NAMES + [
         "aux_out", "out_states", "out_tails", "slot_block", "slot_used",
         "x_send", "x_recv", "aux_send", "aux_recv", "core_send", "core_recv",
-        "st_send", "st_recv", "tl_send", "tl_recv", "own"]
+        "st_send", "st_recv", "tl_send", "tl_recv", "own",
+        "decay_in", "beta_in", "conv_weight", "a_log", "dt_bias", "req_blocks", "replica_of", "finished", "small"]
     for name, ref in zip(names, scratch):
         setattr(s, name, ref)
-    s.conv_weight, s.a_log, s.dt_bias, s.req_blocks = conv_weight, a_log, dt_bias, req_blocks
-    s.replica_of, s.finished = replica_of, finished
+    small = [
+        pltpu.make_async_copy(source, target, s.small.at[n]) for n, (source, target) in enumerate((
+            (decay_in, s.decay_in), (beta_in, s.beta_in), (conv_weight, s.conv_weight), (a_log, s.a_log),
+            (dt_bias, s.dt_bias), (req_blocks, s.req_blocks), (replica_of, s.replica_of), (finished, s.finished)))]
+    for copy in small:
+        copy.start()
     me, rep = lax.axis_index("seq"), lax.axis_index("rep")
 
     barrier = pltpu.get_barrier_semaphore()
@@ -228,9 +260,11 @@
         pl.semaphore_signal(barrier, inc=1, device_id={"seq": lax.rem(me + k, N_SEQ)}, device_id_type=MESH)
     for k in range(1, N_REP):
         pl.semaphore_signal(barrier, inc=1, device_id={"rep": lax.rem(rep + k, N_REP)}, device_id_type=MESH)
+    for copy in small:
+        copy.wait()
     for h in range(N_SEQ):
-        s.aux_out[h, 0:2, :] = decay_in[0, h].astype(f32)
-        s.aux_out[h, 2:4, :] = beta_in[0, h].astype(f32)
+        s.aux_out[h, 0:2, :] = s.decay_in[0, h].astype(f32)
+        s.aux_out[h, 2:4, :] = s.beta_in[0, h].astype(f32)
         s.aux_out[h, 4:8, :] = jnp.zeros((4, T), f32)
 
     own_x = pltpu.make_async_copy(mixed.at[0, me], s.x.at[me], s.own.at[0])
@@ -251,12 +285,13 @@
             src_ref=mixed.at[0, to], dst_ref=s.x.at[me], send_sem=s.x_send.at[k], recv_sem=s.x_recv.at[k],
             device_id={"seq": to}, device_id_type=MESH)
 
-    def start_inputs(k, carry):
+    def start_aux(k, carry):
         aux_copy(k).start()
-        x_copy(k).start()
-        return carry
-
-    lax.fori_loop(1, N_SEQ, start_inputs, 0)
+        return carry
+
+    lax.fori_loop(1, N_SEQ, start_aux, 0)
+    for n in range(AHEAD):
+        x_copy(ORDER[n]).start()
     setup_tables(s)
     fill_slots(s)
     own_x.wait()
@@ -269,15 +304,19 @@
     lax.fori_loop(1, N_SEQ, wait_aux, 0)
     setup_gates(s)
 
-    def prep(k, carry):
-        @pl.when(k < N_SEQ)
-        def _():
-            x_copy(k).wait_recv()
-
-        prep_chunk(s, lax.rem(me + k, N_SEQ))
-        return carry
-
-    lax.fori_loop(1, N_SEQ + 1, prep, 0)
+    def prep(g, carry):
+        for n in range(4):
+            @pl.when(g == n)
+            def _(n=n):
+                for m in range(READY[n], READY[n + 1]):
+                    x_copy(ORDER[m]).wait_recv()
+                    if m + AHEAD < N_SEQ - 1:
+                        x_copy(ORDER[m + AHEAD]).start()
+
+        prep_chunks(s, [lax.rem(me + entry([group[t] for group in GROUPS], g), N_SEQ) for t in range(4)])
+        return carry
+
+    lax.fori_loop(0, 4, prep, 0)
     scan_blocks(s)
 
     def core_copy(k):
@@ -296,27 +335,28 @@
                 src_ref=s.out_tails.at[to], dst_ref=got_tails.at[rep], send_sem=s.tl_send.at[k],
                 recv_sem=s.tl_recv.at[k], device_id={"rep": to}, device_id_type=MESH)]
 
-    def post(k, carry):
-        for half in range(2):
-            j = 2 * k - 1 + half
-            post_chunk(s, lax.rem(me + j, N_SEQ))
-
-            @pl.when(j < N_SEQ)
-            def _():
-                core_copy(j).start()
-
-        d = lax.rem(rep + k, N_REP)
-        tails = [build_slot(s, d, slot) for slot in range(CAP)]
-        s.out_tails[d] = jnp.concatenate(tails, axis=0).astype(bf16)
-
-        @pl.when(k < N_REP)
-        def _():
-            for copy in state_copies(k):
-                copy.start()
-
-        return carry
-
-    lax.fori_loop(1, N_REP + 1, post, 0)
+    def post(g, carry):
+        steps = [entry([(ORDER + (0,))[4 * n + t] for n in range(4)], g) for t in range(4)]
+        post_chunks(s, [lax.rem(me + k, N_SEQ) for k in steps])
+        for t in range(4):
+            @pl.when(steps[t] > 0)
+            def _(t=t):
+                core_copy(steps[t]).start()
+
+        for t in range(2):
+            k = entry([REP_ORDER[2 * n + t] for n in range(4)], g)
+            d = lax.rem(rep + k, N_REP)
+            tails = [build_slot(s, d, slot) for slot in range(CAP)]
+            s.out_tails[d] = jnp.concatenate(tails, axis=0).astype(bf16)
+
+            @pl.when(k > 0)
+            def _(k=k):
+                for copy in state_copies(k):
+                    copy.start()
+
+        return carry
+
+    lax.fori_loop(0, 4, post, 0)
     own = [
         pltpu.make_async_copy(s.core.at[me], back.at[me], s.own.at[2]),
         pltpu.make_async_copy(s.out_states.at[rep], got_states.at[rep], s.own.at[3]),
@@ -385,14 +425,18 @@
             jax.ShapeDtypeStruct((N_SEQ, 2 * T, T), bf16),
             jax.ShapeDtypeStruct((N_REP, CAP, 2, T, T), bf16),
             jax.ShapeDtypeStruct((N_REP, 16, 512), bf16)],
-        in_specs=[ANY, VMEM, VMEM, VMEM] + [SMEM] * 5,
+        in_specs=[ANY] * 9,
         out_specs=[ANY] * 3,
         scratch_shapes=[pltpu.VMEM(*SCRATCH[name]) for name in SCRATCH_NAMES] + [
             pltpu.VMEM((N_SEQ, 8, T), f32),
             pltpu.VMEM((N_REP, CAP, 2, T, T), bf16),
             pltpu.VMEM((N_REP, 16, 512), bf16),
             pltpu.SMEM((N_REP * CAP,), jnp.int32),
-            pltpu.SMEM((N_REP * CAP,), jnp.int32)] + [dma((N_SEQ,))] * 6 + [dma((N_REP,))] * 4 + [dma((5,))],
+            pltpu.SMEM((N_REP * CAP,), jnp.int32)] + [dma((N_SEQ,))] * 6 + [dma((N_REP,))] * 4 + [
+                dma((5,)),
+                pltpu.VMEM(decay_in.shape, bf16), pltpu.VMEM(beta_in.shape, bf16), pltpu.VMEM(conv_weight.shape, bf16),
+                pltpu.SMEM(a_log.shape, f32), pltpu.SMEM(dt_bias.shape, f32), pltpu.SMEM(req_blocks.shape, jnp.int32),
+                pltpu.SMEM(replica_of.shape, jnp.int32), pltpu.SMEM(finished.shape, jnp.int32), dma((8,))],
         compiler_params=pltpu.CompilerParams(
             collective_id=0, has_side_effects=True, vmem_limit_bytes=48 << 20),
     )(mixed, decay_in, beta_in, conv_weight, a_log, dt_bias, req_blocks, replica_of, finished)

time: 123 us -> 84.8 us (0.69)
  the two profiles are of different devices: /device:TPU:11 before, /device:TPU:0 now
where the time goes in v1:
time: 84.8 us; the launch traced here: 84.3 us
  Pallas kernels  72.6 us (86%)
  local copies, waits for them, and re-layouts  11.1 us (13%)
    pallas_call x1, Pallas kernels, body(): pl.pallas_call(main_kernel, name='main', out_shape=[jax.ShapeDtypeStruct(...  67.7 us
    unnamed x23, local copies, waits for them, and re-layouts  9.56 us
    pallas_call x1, Pallas kernels, body(): pl.pallas_call(finish_kernel, name='finish', grid=(N_SEQ // HEADS,), out_...  4.89 us

profile of v1, /device:TPU:0, one launch (start us, length us, event | category | flops | bytes accessed | tf_op | source)
XLA Modules:
  0.0 84.3 jit_solution(16568748982769087454)
XLA Ops:
  0.6 0.7 copy.14.conv_weight
  1.3 0.0 copy-start
  1.3 1.6 %copy-done = bf16[1,16,512,128]{3,2,1,0:T(8,128)(2,1)S(1)} copy-done((bf16[1,16,512,128]{3,2,1,0:T(8,128)(2,1)S(1)}, bf16[1,16,512,128]{3,2,1,0:T(8,128)(2,1)}, u32[]{:S(2)}) %copy-start) | copy-done | bytes 2097176
  2.9 0.0 copy-start.4
  2.9 0.7 copy-done.4
  3.6 0.0 copy-start.5
  3.6 0.7 copy-done.5
  4.3 0.0 copy-start.6
  4.3 0.7 copy-done.6
  5.0 0.0 copy-start.7
  5.0 0.7 copy-done.7
  5.6 0.0 copy-start.8
  5.6 0.7 copy-done.8
  6.3 0.0 copy-start.9
  6.3 0.7 copy-done.9
  6.9 0.0 copy-start.10
  6.9 0.7 copy-done.10
  7.6 67.7 %main.1 = (bf16[16,256,128]{2,1,0:T(8,128)(2,1)S(1)}, bf16[8,2,2,128,128]{4,3,2,1,0:T(8,128)(2,1)S(1)}, bf16[8,16,512]{2,1,0:T(8,128)(2,1)S(1)}) custom-call(bf16[1,16,512,128]{3,2,1,0:T(8,128)(2,1)S(1)} %copy-done, bf16[1,16,2,128]{3,2,1,0:T(2,128)(2,1)S(1)} %copy-done.4, bf16[1,16,2,128]{3,2,1,0:T(2,128)(2,1)S(1)} %copy-done.5, ...), custom_call_target="tpu_custom_call" | custom-call | tf_op jit(solution)/shard_map/main/pallas_call | solution.py:421
  75.3 0.0 copy-start.1
  75.3 1.0 %copy-done.1 = bf16[16,256,128]{2,1,0:T(8,128)(2,1)} copy-done((bf16[16,256,128]{2,1,0:T(8,128)(2,1)}, bf16[16,256,128]{2,1,0:T(8,128)(2,1)S(1)}, u32[]{:S(2)}) %copy-start.1) | copy-done | bytes 1048600
  76.3 0.0 copy-start.2
  76.3 1.0 %copy-done.2 = bf16[8,2,2,128,128]{4,3,2,1,0:T(8,128)(2,1)} copy-done((bf16[8,2,2,128,128]{4,3,2,1,0:T(8,128)(2,1)}, bf16[8,2,2,128,128]{4,3,2,1,0:T(8,128)(2,1)S(1)}, u32[]{:S(2)}) %copy-start.2) | copy-done | bytes 1048600
  77.3 0.0 copy-start.3
  77.3 0.6 copy-done.3
  77.9 4.9 %finish.1 = (bf16[1,16,256,128]{3,2,1,0:T(8,128)(2,1)}, f32[1,16,2,128,128]{4,3,2,1,0:T(8,128)}, bf16[1,16,3,1,512]{4,3,2,1,0:T(2,128)(2,1)}) custom-call(bf16[16,256,128]{2,1,0:T(8,128)(2,1)} %copy-done.1, bf16[1,16,256,128]{3,2,1,0:T(8,128)(2,1)} %gate.1, f32[1,128]{1,0:T(1,128)} %bitcast.1, bf16[8,2,2,128,128]{4,3,2,1,0:T(8,128)(2,1)} %copy-done.2, ...), custom_call_target="tpu_custom_call" | custom-call | tf_op jit(solution)/shard_map/finish/pallas_call | solution.py:444
  82.8 1.5 %copy.15 = bf16[1,16,3,1,512]{4,1,3,2,0:T(8,128)(2,1)} copy(bf16[1,16,3,1,512]{4,3,2,1,0:T(2,128)(2,1)} %get-tuple-element.11) | data formatting | bytes 98304 | tf_op jit(solution)/shard_map/finish/pallas_call | solution.py:444
Async XLA Ops:
  1.3 1.6 %copy-start = (bf16[1,16,512,128]{3,2,1,0:T(8,128)(2,1)S(1)}, bf16[1,16,512,128]{3,2,1,0:T(8,128)(2,1)}, u32[]{:S(2)}) copy-start(bf16[1,16,512,128]{3,2,1,0:T(8,128)(2,1)} %mixed.1) | copy-start | bytes 6291460
  2.9 0.7 copy-start.4
  3.6 0.7 copy-start.5
  4.3 0.7 copy-start.6
  5.0 0.7 copy-start.7
  5.6 0.7 copy-start.8
  6.3 0.7 copy-start.9
  6.9 0.7 copy-start.10
  75.3 1.0 %copy-start.1 = (bf16[16,256,128]{2,1,0:T(8,128)(2,1)}, bf16[16,256,128]{2,1,0:T(8,128)(2,1)S(1)}, u32[]{:S(2)}) copy-start(bf16[16,256,128]{2,1,0:T(8,128)(2,1)S(1)} %get-tuple-element.6.back) | copy-start | bytes 3145732
  76.3 1.0 %copy-start.2 = (bf16[8,2,2,128,128]{4,3,2,1,0:T(8,128)(2,1)}, bf16[8,2,2,128,128]{4,3,2,1,0:T(8,128)(2,1)S(1)}, u32[]{:S(2)}) copy-start(bf16[8,2,2,128,128]{4,3,2,1,0:T(8,128)(2,1)S(1)} %get-tuple-element.7.got_states) | copy-start | bytes 3145732
  77.3 0.6 copy-start.3

commit v2 on v1

--- a/solution.py
+++ b/solution.py
@@ -185,11 +185,13 @@
 
 
 N_SEQ, N_REP, REQS, CAP = 16, 8, 8, 2
-AHEAD = 8
+AHEAD = 11
+FIRST = False
+VMEM_GRANT = 63 << 20
 MESH = pl.DeviceIdType.MESH
 VMEM = pl.BlockSpec(memory_space=pltpu.VMEM)
 SMEM = pl.BlockSpec(memory_space=pltpu.SMEM)
-ANY = pl.BlockSpec(memory_space=pl.ANY)
+HBM = pl.BlockSpec(memory_space=pltpu.MemorySpace.HBM)
 SCRATCH_NAMES = list(SCRATCH)
 
 
@@ -335,6 +337,18 @@
                 src_ref=s.out_tails.at[to], dst_ref=got_tails.at[rep], send_sem=s.tl_send.at[k],
                 recv_sem=s.tl_recv.at[k], device_id={"rep": to}, device_id_type=MESH)]
 
+    def hand_off(g):
+        for t in range(2):
+            k = entry([REP_ORDER[2 * n + t] for n in range(4)], g)
+            d = lax.rem(rep + k, N_REP)
+            tails = [build_slot(s, d, slot) for slot in range(CAP)]
+            s.out_tails[d] = jnp.concatenate(tails, axis=0).astype(bf16)
+
+            @pl.when(k > 0)
+            def _(k=k):
+                for copy in state_copies(k):
+                    copy.start()
+
     def post(g, carry):
         steps = [entry([(ORDER + (0,))[4 * n + t] for n in range(4)], g) for t in range(4)]
         post_chunks(s, [lax.rem(me + k, N_SEQ) for k in steps])
@@ -343,19 +357,16 @@
             def _(t=t):
                 core_copy(steps[t]).start()
 
-        for t in range(2):
-            k = entry([REP_ORDER[2 * n + t] for n in range(4)], g)
-            d = lax.rem(rep + k, N_REP)
-            tails = [build_slot(s, d, slot) for slot in range(CAP)]
-            s.out_tails[d] = jnp.concatenate(tails, axis=0).astype(bf16)
-
-            @pl.when(k > 0)
-            def _(k=k):
-                for copy in state_copies(k):
-                    copy.start()
-
-        return carry
-
+        if not FIRST:
+            hand_off(g)
+        return carry
+
+    def hand_off_first(g, carry):
+        hand_off(g)
+        return carry
+
+    if FIRST:
+        lax.fori_loop(0, 4, hand_off_first, 0)
     lax.fori_loop(0, 4, post, 0)
     own = [
         pltpu.make_async_copy(s.core.at[me], back.at[me], s.own.at[2]),
@@ -381,39 +392,88 @@
         copy.wait()
 
 
-HEADS = 4
-
-
-def finish_kernel(back, gate, gain, got_states, got_tails, mixer, states, tails):
-    step = pl.program_id(0)
-    column = jnp.broadcast_to(gain[...], (T, T)).T
-    for h in range(HEADS):
-        for r in range(2):
-            rows = slice(r * T, (r + 1) * T)
-            value = back[h, rows, :].astype(f32)
-            inverse = lax.rsqrt(jnp.mean(value * value, axis=0, keepdims=True) + 1e-6)
-            z = gate[0, h, rows, :].astype(f32)
-            mixer[0, h, rows, :] = (value * inverse * column * (z / (1.0 + jnp.exp(-z)))).astype(bf16)
+def finish_kernel(back_hbm, gate, gain_hbm, got_states_hbm, got_tails_hbm, mixer, states, tails_out,
+                  z_in, mixed_out, states_out, back, gain, got_states, got_tails, tails,
+                  gate_sem, back_sem, mixer_sem, states_sem, load_sem):
+    first = [
+        pltpu.make_async_copy(got_tails_hbm, got_tails, load_sem.at[0]),
+        pltpu.make_async_copy(got_states_hbm, got_states, load_sem.at[1]),
+        pltpu.make_async_copy(gain_hbm, gain, load_sem.at[2])]
+
+    def load(h):
+        return [
+            pltpu.make_async_copy(gate.at[0, h], z_in.at[h], gate_sem.at[h]),
+            pltpu.make_async_copy(back_hbm.at[h], back.at[h], back_sem.at[h])]
+
+    for copy in first:
+        copy.start()
+    for h in range(N_SEQ):
+        for copy in load(h):
+            copy.start()
+    for copy in first:
+        copy.wait()
     counts = [jnp.max(got_tails[q, 0:8, 0:T].astype(f32)[3:4]).astype(jnp.int32) for q in range(N_REP)]
     bases, base = [], jnp.int32(0)
     for q in range(N_REP):
         bases.append(base)
         base = base + counts[q]
-    for h in range(HEADS):
-        slot = step * HEADS + h
+
+    def store_states(slot):
+        return pltpu.make_async_copy(states_out.at[slot], states.at[0, slot], states_sem.at[slot])
+
+    def store_mixer(h):
+        return pltpu.make_async_copy(mixed_out.at[h], mixer.at[0, h], mixer_sem.at[h])
+
+    def land(slot):
         pick, used = jnp.int32(0), jnp.int32(0)
         for q in range(N_REP):
-            for k in range(CAP):
-                hit = (bases[q] + k == slot) & (counts[q] > k)
-                pick = pick + jnp.where(hit, q * CAP + k, 0)
-                used = used + jnp.where(hit, 1, 0)
+            rank = slot - bases[q]
+            hit = (rank >= 0) & (rank < counts[q])
+            pick = jnp.where(hit, q * CAP + rank, pick)
+            used = jnp.where(hit, 1, used)
         scale = used.astype(f32)
         source, rank = pick // CAP, pick % CAP
         for r in range(2):
-            states[0, h, r] = got_states[source, rank, r].astype(f32) * scale
+            states_out[slot, r] = got_states[source, rank, r].astype(f32) * scale
+        store_states(slot).start()
         both = got_tails[source].astype(f32)
         rows = jnp.where(rank == 0, both[0:8], both[8:16]) * scale
-        tails[0, h, :, 0, :] = rows[0:3].astype(bf16)
+        for p in range(3):
+            tails[p, pl.ds(slot, 1), :] = rows[p:p + 1]
+
+    def land_some(g, carry):
+        for t in range(4):
+            land(g * 4 + t)
+        return carry
+
+    lax.fori_loop(0, N_REP * CAP // 4, land_some, 0)
+    tails_out[...] = tails[...].astype(bf16)
+    column = jnp.broadcast_to(gain[...], (T, T)).T
+
+    def norm(g, carry):
+        for t in range(4):
+            for copy in load(g * 4 + t):
+                copy.wait()
+        for t in range(4):
+            h = g * 4 + t
+            for r in range(2):
+                rows = slice(r * T, (r + 1) * T)
+                value = back[h, rows, :].astype(f32)
+                inverse = lax.rsqrt(jnp.mean(value * value, axis=0, keepdims=True) + 1e-6)
+                z = z_in[h, rows, :].astype(f32)
+                mixed_out[h, rows, :] = (value * inverse * column * (z / (1.0 + jnp.exp(-z)))).astype(bf16)
+        for t in range(4):
+            store_mixer(g * 4 + t).start()
+        return carry
+
+    lax.fori_loop(0, N_SEQ // 4, norm, 0)
+
+    def drain(h, carry):
+        store_states(h).wait()
+        store_mixer(h).wait()
+        return carry
+
+    lax.fori_loop(0, N_SEQ, drain, 0)
 
 
 def body(mixed, decay_in, beta_in, gate_z, conv_weight, a_log, dt_bias, norm_gain, req_blocks, replica_of, finished):
@@ -425,8 +485,8 @@
             jax.ShapeDtypeStruct((N_SEQ, 2 * T, T), bf16),
             jax.ShapeDtypeStruct((N_REP, CAP, 2, T, T), bf16),
             jax.ShapeDtypeStruct((N_REP, 16, 512), bf16)],
-        in_specs=[ANY] * 9,
-        out_specs=[ANY] * 3,
+        in_specs=[HBM] * 9,
+        out_specs=[HBM] * 3,
         scratch_shapes=[pltpu.VMEM(*SCRATCH[name]) for name in SCRATCH_NAMES] + [
             pltpu.VMEM((N_SEQ, 8, T), f32),
             pltpu.VMEM((N_REP, CAP, 2, T, T), bf16),
@@ -434,32 +494,34 @@
             pltpu.SMEM((N_REP * CAP,), jnp.int32),
             pltpu.SMEM((N_REP * CAP,), jnp.int32)] + [dma((N_SEQ,))] * 6 + [dma((N_REP,))] * 4 + [
                 dma((5,)),
-                pltpu.VMEM(decay_in.shape, bf16), pltpu.VMEM(beta_in.shape, bf16), pltpu.VMEM(conv_weight.shape, bf16),
+                pltpu.VMEM(decay_in.shape, bf16), pltpu.VMEM(beta_in.shape, bf16), pltpu.VMEM((1, 4, 512), bf16),
                 pltpu.SMEM(a_log.shape, f32), pltpu.SMEM(dt_bias.shape, f32), pltpu.SMEM(req_blocks.shape, jnp.int32),
                 pltpu.SMEM(replica_of.shape, jnp.int32), pltpu.SMEM(finished.shape, jnp.int32), dma((8,))],
         compiler_params=pltpu.CompilerParams(
-            collective_id=0, has_side_effects=True, vmem_limit_bytes=48 << 20),
-    )(mixed, decay_in, beta_in, conv_weight, a_log, dt_bias, req_blocks, replica_of, finished)
-    whole = lambda shape: pl.BlockSpec(shape, lambda i: (0,) * len(shape))
+            collective_id=0, has_side_effects=True, vmem_limit_bytes=VMEM_GRANT),
+    )(mixed, decay_in, beta_in, jnp.transpose(conv_weight, (1, 0, 2)), a_log, dt_bias, req_blocks, replica_of, finished)
     mixer, states, tails = pl.pallas_call(
         finish_kernel,
         name="finish",
-        grid=(N_SEQ // HEADS,),
         out_shape=[
             jax.ShapeDtypeStruct((1, N_SEQ, 2 * T, T), bf16),
             jax.ShapeDtypeStruct((1, N_REP * CAP, 2, T, T), f32),
-            jax.ShapeDtypeStruct((1, N_REP * CAP, 3, 1, 512), bf16)],
-        in_specs=[
-            pl.BlockSpec((HEADS, 2 * T, T), lambda i: (i, 0, 0)),
-            pl.BlockSpec((1, HEADS, 2 * T, T), lambda i: (0, i, 0, 0)),
-            whole((1, T)),
-            whole((N_REP, CAP, 2, T, T)),
-            whole((N_REP, 16, 512))],
-        out_specs=[
-            pl.BlockSpec((1, HEADS, 2 * T, T), lambda i: (0, i, 0, 0)),
-            pl.BlockSpec((1, HEADS, 2, T, T), lambda i: (0, i, 0, 0, 0)),
-            pl.BlockSpec((1, HEADS, 3, 1, 512), lambda i: (0, i, 0, 0, 0))],
+            jax.ShapeDtypeStruct((3, N_REP * CAP, 512), bf16)],
+        in_specs=[HBM] * 5,
+        out_specs=[HBM, HBM, VMEM],
+        scratch_shapes=[
+            pltpu.VMEM((N_SEQ, 2 * T, T), bf16),
+            pltpu.VMEM((N_SEQ, 2 * T, T), bf16),
+            pltpu.VMEM((N_REP * CAP, 2, T, T), f32),
+            pltpu.VMEM((N_SEQ, 2 * T, T), bf16),
+            pltpu.VMEM((1, T), f32),
+            pltpu.VMEM((N_REP, CAP, 2, T, T), bf16),
+            pltpu.VMEM((N_REP, 16, 512), bf16),
+            pltpu.VMEM((3, N_REP * CAP, 512), f32),
+            dma((N_SEQ,)), dma((N_SEQ,)), dma((N_SEQ,)), dma((N_REP * CAP,)), dma((3,))],
+        compiler_params=pltpu.CompilerParams(vmem_limit_bytes=VMEM_GRANT),
     )(back, gate_z, norm_gain.reshape(1, T), got_states, got_tails)
+    tails = jnp.transpose(tails, (1, 0, 2))[None, :, :, None, :]
     return mixer, states, tails
 
 

time: 84.8 us -> 73.4 us (0.87)
  local copies, waits for them, and re-layouts: 11.1 us -> 0 us
  Pallas kernels: 72.6 us -> 71.6 us
    unnamed x23 -> x0, local copies, waits for them, and re-layouts: 9.56 us -> none
    pallas_call x1, Pallas kernels: 67.7 us -> 66 us  [body(): pl.pallas_call(main_kernel, name='main', out_shape=[jax.ShapeDtypeStruct(...]
    pallas_call x1 -> x0, local copies, waits for them, and re-layouts: 1.52 us -> none  [body(): pl.pallas_call(finish_kernel, name='finish', grid=(N_SEQ // HEADS,), out_...]
where the time goes in v2:
time: 73.4 us; the launch traced here: 72.3 us
  Pallas kernels  71.6 us (98%)
    pallas_call x1, Pallas kernels, body(): pl.pallas_call(main_kernel, name='main', out_shape=[jax.ShapeDtypeStruct(...  66 us
    pallas_call x1, Pallas kernels, body(): pl.pallas_call(finish_kernel, name='finish', out_shape=[jax.ShapeDtypeStr...  5.63 us

profile of v2, /device:TPU:0, one launch (start us, length us, event | category | flops | bytes accessed | tf_op | source)
XLA Modules:
  0.0 72.3 jit_solution(17331643599737160534)
XLA Ops:
  0.6 66.0 %main.1 = (bf16[16,256,128]{2,1,0:T(8,128)(2,1)}, bf16[8,2,2,128,128]{4,3,2,1,0:T(8,128)(2,1)}, bf16[8,16,512]{2,1,0:T(8,128)(2,1)}) custom-call(bf16[1,16,512,128]{3,2,1,0:T(8,128)(2,1)} %mixed.1, bf16[1,16,2,128]{3,2,1,0:T(2,128)(2,1)} %decay_in.1, bf16[1,16,2,128]{3,2,1,0:T(2,128)(2,1)} %beta_in.1, bf16[1,4,512]{2,1,0:T(4,128)(2,1)} %bitcast.7, f32[2]{0:T(128)} %a_log.1, ...), custom_call_target="tpu_custom_call" | custom-call | tf_op jit(solution)/shard_map/main/pallas_call | solution.py:481
  66.6 5.6 %finish.1 = (bf16[1,16,256,128]{3,2,1,0:T(8,128)(2,1)}, f32[1,16,2,128,128]{4,3,2,1,0:T(8,128)}, bf16[3,16,512]{2,1,0:T(8,128)(2,1)}) custom-call(bf16[16,256,128]{2,1,0:T(8,128)(2,1)} %get-tuple-element.9.back_hbm, bf16[1,16,256,128]{3,2,1,0:T(8,128)(2,1)} %gate.1, f32[1,128]{1,0:T(1,128)} %bitcast.8, ...), custom_call_target="tpu_custom_call" | custom-call | tf_op jit(solution)/shard_map/finish/pallas_call | solution.py:503

commit v3 on v2

--- a/solution.py
+++ b/solution.py
@@ -113,59 +113,77 @@
     return [(u[m].astype(f32) + dot(u[m], res[m])).astype(bf16) for m in count]
 
 
-def weigh(s, c, data, u):
-    qT, kT, k, values, _ = data
+def weigh(s, chunks, data, u):
     zero = jnp.zeros((SPAN, T), bf16)
-    kk = jnp.concatenate([
-        jnp.concatenate([k[:SPAN], zero], axis=0),
-        jnp.concatenate([zero, k[SPAN:]], axis=0)], axis=1)
-    for r in range(2):
-        beta = row(s.beta.at[r], c)
-        sk = (kT.astype(f32) * (beta * row(s.lift.at[r], c))).astype(bf16)
-        sv = (values[r].astype(f32) * beta).astype(bf16)
-        w = dot(jnp.concatenate([sv, sk], axis=0), u[r])
-        wb = w.astype(bf16)
+    pairs = [(m, r) for m in range(len(chunks)) for r in range(2)]
+    kk, left, fade, stay, keep0, keep1 = [], [], [], [], [], []
+    for m, c in enumerate(chunks):
+        qT, kT, k, values, _ = data[m]
+        kk.append(jnp.concatenate([
+            jnp.concatenate([k[:SPAN], zero], axis=0),
+            jnp.concatenate([zero, k[SPAN:]], axis=0)], axis=1))
+        for r in range(2):
+            beta = row(s.beta.at[r], c)
+            sk = (kT.astype(f32) * (beta * row(s.lift.at[r], c))).astype(bf16)
+            sv = (values[r].astype(f32) * beta).astype(bf16)
+            left.append(jnp.concatenate([sv, sk], axis=0))
+            fade.append(row(s.fade.at[r], c))
+            stay.append(row(s.stay, 2 * c + 1))
+            keep0.append(row(s.keep.at[r, 0], c))
+            keep1.append(row(s.keep.at[r, 1], c))
+    w = [dot(left[n], u[n]) for n in range(len(pairs))]
+    gw = [dot((w[n] * fade[n]).astype(bf16), kk[m]) for n, (m, r) in enumerate(pairs)]
+    joined = [g[:, :T].astype(bf16) for g in gw]
+    both = [dot(joined[n], gw[n][T:, T:].astype(bf16)) for n in range(len(pairs))]
+    for n, (m, r) in enumerate(pairs):
+        c, g = chunks[m], gw[n]
+        wb = w[n].astype(bf16)
         s.wv[c, r] = wb[:T]
         s.wq[c, r, :, :T] = wb[T:]
-        s.wq[c, r, :, T:] = qT
-        gw = dot((w * row(s.fade.at[r], c)).astype(bf16), kk)
-        for b in range(2):
-            s.add[c, r, b] = gw[:T, b * T:(b + 1) * T]
-            s.turn[c, r, b] = gw[T:, b * T:(b + 1) * T].astype(bf16)
+        s.wq[c, r, :, T:] = data[m][0]
+        s.add[c, r, 0] = g[:T, :T]
+        s.add[c, r, 1] = g[:T, T:] + stay[n] * (keep1[n] * g[:T, :T] - both[n][:T])
+        s.turn[c, r, :, :T] = joined[n][T:]
+        s.turn[c, r, :, T:] = (stay[n] * (keep1[n] * g[T:, :T] + keep0[n] * g[T:, T:] - both[n][T:])).astype(bf16)
 
 
 def prep_chunks(s, chunks):
     data = [read_chunk(s, c) for c in chunks]
     minus = [n for d in data for n in d[4]]
     u = solve(s, minus)
-    for m, c in enumerate(chunks):
-        weigh(s, c, data[m], u[2 * m:2 * m + 2])
+    weigh(s, chunks, data, u)
 
 def scan_blocks(s):
     def step(c, carry):
         state = list(carry)
-        for b in range(2):
-            stay = row(s.stay, 2 * c + b)
-            for r in range(2):
-                inside = state[r] * stay
-                low = inside.astype(bf16)
-                s.enter[c, r, b * T:(b + 1) * T, :] = low
-                state[r] = (row(s.keep.at[r, b], c) * inside + s.add[c, r, b]) - dot(low, s.turn[c, r, b])
-                s.leave[2 * c + b, r] = state[r].astype(bf16)
+        stay0, stay1 = row(s.stay, 2 * c), row(s.stay, 2 * c + 1)
+        for r in range(2):
+            keep0, keep1 = row(s.keep.at[r, 0], c), row(s.keep.at[r, 1], c)
+            inside = state[r] * stay0
+            low = inside.astype(bf16)
+            moved = dot(low, s.turn[c, r])
+            state[r] = (stay1 * keep0 * keep1 * inside + s.add[c, r, 1]) - moved[:, T:]
+            middle = (keep0 * inside + s.add[c, r, 0]) - moved[:, :T]
+            s.enter[c, r, :T, :] = low
+            s.enter[c, r, T:, :] = (middle * stay1).astype(bf16)
+            s.leave[2 * c, r] = middle.astype(bf16)
+            s.leave[2 * c + 1, r] = state[r].astype(bf16)
         return tuple(state)
+
     zero = jnp.zeros((T, T), f32)
     lax.fori_loop(0, NC, step, (zero, zero))
 
+
 def post_chunks(s, chunks):
     first = iota((1, T), 1) < SPAN
-    for c in chunks:
-        for r in range(2):
-            both = dot(s.enter[c, r], s.wq[c, r])
-            seenk = jnp.where(first, both[:T, :T], both[T:, :T])
-            seenq = jnp.where(first, both[:T, T:], both[T:, T:])
-            new = (s.wv[c, r].astype(f32) - seenk).astype(bf16)
-            out = row(s.lift.at[r], c) * seenq + dot(new, s.score[c, r])
-            s.core[c, r * T:(r + 1) * T, :] = out.astype(bf16)
+    pairs = [(c, r) for c in chunks for r in range(2)]
+    both = [dot(s.enter[c, r], s.wq[c, r]) for c, r in pairs]
+    new = [(s.wv[c, r].astype(f32) - jnp.where(first, x[:T, :T], x[T:, :T])).astype(bf16)
+           for (c, r), x in zip(pairs, both)]
+    old = [row(s.lift.at[r], c) * jnp.where(first, x[:T, T:], x[T:, T:]) for (c, r), x in zip(pairs, both)]
+    out = [(old[n] + dot(new[n], s.score[c, r])).astype(bf16) for n, (c, r) in enumerate(pairs)]
+    for n, (c, r) in enumerate(pairs):
+        s.core[c, r * T:(r + 1) * T, :] = out[n]
 
 
 SCRATCH = dict(
@@ -175,7 +193,7 @@
     seen=((T, T), f32), later=((T, T), f32), eye=((T, T), f32), level=((6, T, T), bf16),
     taps=((4, 512, T), f32),
     wv=((NC, 2, T, T), bf16), wq=((NC, 2, T, 2 * T), bf16), score=((NC, 2, T, T), bf16),
-    add=((NC, 2, 2, T, T), f32), turn=((NC, 2, 2, T, T), bf16),
+    add=((NC, 2, 2, T, T), f32), turn=((NC, 2, T, 2 * T), bf16),
     enter=((NC, 2, 2 * T, T), bf16), leave=((32, 2, T, T), bf16),
     core=((NC, 256, T), bf16), tails=((32, 8, 512), f32),
 )
@@ -186,6 +204,7 @@
 
 N_SEQ, N_REP, REQS, CAP = 16, 8, 8, 2
 AHEAD = 11
+BEFORE = 4
 FIRST = False
 VMEM_GRANT = 63 << 20
 MESH = pl.DeviceIdType.MESH
@@ -249,19 +268,41 @@
         "decay_in", "beta_in", "conv_weight", "a_log", "dt_bias", "req_blocks", "replica_of", "finished", "small"]
     for name, ref in zip(names, scratch):
         setattr(s, name, ref)
+    me, rep = lax.axis_index("seq"), lax.axis_index("rep")
+
+    barrier = pltpu.get_barrier_semaphore()
+    for k in range(1, N_SEQ):
+        pl.semaphore_signal(barrier, inc=1, device_id={"seq": lax.rem(me + k, N_SEQ)}, device_id_type=MESH)
+    for k in range(1, N_REP):
+        pl.semaphore_signal(barrier, inc=1, device_id={"rep": lax.rem(rep + k, N_REP)}, device_id_type=MESH)
     small = [
         pltpu.make_async_copy(source, target, s.small.at[n]) for n, (source, target) in enumerate((
             (decay_in, s.decay_in), (beta_in, s.beta_in), (conv_weight, s.conv_weight), (a_log, s.a_log),
             (dt_bias, s.dt_bias), (req_blocks, s.req_blocks), (replica_of, s.replica_of), (finished, s.finished)))]
     for copy in small:
         copy.start()
-    me, rep = lax.axis_index("seq"), lax.axis_index("rep")
-
-    barrier = pltpu.get_barrier_semaphore()
-    for k in range(1, N_SEQ):
-        pl.semaphore_signal(barrier, inc=1, device_id={"seq": lax.rem(me + k, N_SEQ)}, device_id_type=MESH)
-    for k in range(1, N_REP):
-        pl.semaphore_signal(barrier, inc=1, device_id={"rep": lax.rem(rep + k, N_REP)}, device_id_type=MESH)
+    own_x = pltpu.make_async_copy(mixed.at[0, me], s.x.at[me], s.own.at[0])
+    own_x.start()
+
+    def aux_copy(k):
+        to = lax.rem(me + N_SEQ - k, N_SEQ)
+        return pltpu.make_async_remote_copy(
+            src_ref=s.aux_out.at[to], dst_ref=s.aux.at[me], send_sem=s.aux_send.at[k], recv_sem=s.aux_recv.at[k],
+            device_id={"seq": to}, device_id_type=MESH)
+
+    def x_copy(k):
+        to = lax.rem(me + N_SEQ - k, N_SEQ)
+        return pltpu.make_async_remote_copy(
+            src_ref=mixed.at[0, to], dst_ref=s.x.at[me], send_sem=s.x_send.at[k], recv_sem=s.x_recv.at[k],
+            device_id={"seq": to}, device_id_type=MESH)
+
+    def start_aux(k, carry):
+        aux_copy(k).start()
+        return carry
+
+    pl.semaphore_wait(barrier, N_SEQ + N_REP - 2)
+    for n in range(BEFORE):
+        x_copy(ORDER[n]).start()
     for copy in small:
         copy.wait()
     for h in range(N_SEQ):
@@ -269,30 +310,10 @@
         s.aux_out[h, 2:4, :] = s.beta_in[0, h].astype(f32)
         s.aux_out[h, 4:8, :] = jnp.zeros((4, T), f32)
 
-    own_x = pltpu.make_async_copy(mixed.at[0, me], s.x.at[me], s.own.at[0])
     own_aux = pltpu.make_async_copy(s.aux_out.at[me], s.aux.at[me], s.own.at[1])
-    own_x.start()
     own_aux.start()
-    pl.semaphore_wait(barrier, N_SEQ + N_REP - 2)
-
-    def aux_copy(k):
-        to = lax.rem(me + N_SEQ - k, N_SEQ)
-        return pltpu.make_async_remote_copy(
-            src_ref=s.aux_out.at[to], dst_ref=s.aux.at[me], send_sem=s.aux_send.at[k], recv_sem=s.aux_recv.at[k],
-            device_id={"seq": to}, device_id_type=MESH)
-
-    def x_copy(k):
-        to = lax.rem(me + N_SEQ - k, N_SEQ)
-        return pltpu.make_async_remote_copy(
-            src_ref=mixed.at[0, to], dst_ref=s.x.at[me], send_sem=s.x_send.at[k], recv_sem=s.x_recv.at[k],
-            device_id={"seq": to}, device_id_type=MESH)
-
-    def start_aux(k, carry):
-        aux_copy(k).start()
-        return carry
-
     lax.fori_loop(1, N_SEQ, start_aux, 0)
-    for n in range(AHEAD):
+    for n in range(BEFORE, AHEAD):
         x_copy(ORDER[n]).start()
     setup_tables(s)
     fill_slots(s)
@@ -474,6 +495,31 @@
         return carry
 
     lax.fori_loop(0, N_SEQ, drain, 0)
+
+
+def finish_call(*operands):
+    dma = pltpu.SemaphoreType.DMA
+    return pl.pallas_call(
+        finish_kernel,
+        name="finish",
+        out_shape=[
+            jax.ShapeDtypeStruct((1, N_SEQ, 2 * T, T), bf16),
+            jax.ShapeDtypeStruct((1, N_REP * CAP, 2, T, T), f32),
+            jax.ShapeDtypeStruct((3, N_REP * CAP, 512), bf16)],
+        in_specs=[HBM] * 5,
+        out_specs=[HBM, HBM, VMEM],
+        scratch_shapes=[
+            pltpu.VMEM((N_SEQ, 2 * T, T), bf16),
+            pltpu.VMEM((N_SEQ, 2 * T, T), bf16),
+            pltpu.VMEM((N_REP * CAP, 2, T, T), f32),
+            pltpu.VMEM((N_SEQ, 2 * T, T), bf16),
+            pltpu.VMEM((1, T), f32),
+            pltpu.VMEM((N_REP, CAP, 2, T, T), bf16),
+            pltpu.VMEM((N_REP, 16, 512), bf16),
+            pltpu.VMEM((3, N_REP * CAP, 512), f32),
+            dma((N_SEQ,)), dma((N_SEQ,)), dma((N_SEQ,)), dma((N_REP * CAP,)), dma((3,))],
+        compiler_params=pltpu.CompilerParams(vmem_limit_bytes=VMEM_GRANT),
+    )(*operands)
 
 
 def body(mixed, decay_in, beta_in, gate_z, conv_weight, a_log, dt_bias, norm_gain, req_blocks, replica_of, finished):
@@ -500,27 +546,7 @@
         compiler_params=pltpu.CompilerParams(
             collective_id=0, has_side_effects=True, vmem_limit_bytes=VMEM_GRANT),
     )(mixed, decay_in, beta_in, jnp.transpose(conv_weight, (1, 0, 2)), a_log, dt_bias, req_blocks, replica_of, finished)
-    mixer, states, tails = pl.pallas_call(
-        finish_kernel,
-        name="finish",
-        out_shape=[
-            jax.ShapeDtypeStruct((1, N_SEQ, 2 * T, T), bf16),
-            jax.ShapeDtypeStruct((1, N_REP * CAP, 2, T, T), f32),
-            jax.ShapeDtypeStruct((3, N_REP * CAP, 512), bf16)],
-        in_specs=[HBM] * 5,
-        out_specs=[HBM, HBM, VMEM],
-        scratch_shapes=[
-            pltpu.VMEM((N_SEQ, 2 * T, T), bf16),
-            pltpu.VMEM((N_SEQ, 2 * T, T), bf16),
-            pltpu.VMEM((N_REP * CAP, 2, T, T), f32),
-            pltpu.VMEM((N_SEQ, 2 * T, T), bf16),
-            pltpu.VMEM((1, T), f32),
-            pltpu.VMEM((N_REP, CAP, 2, T, T), bf16),
-            pltpu.VMEM((N_REP, 16, 512), bf16),
-            pltpu.VMEM((3, N_REP * CAP, 512), f32),
-            dma((N_SEQ,)), dma((N_SEQ,)), dma((N_SEQ,)), dma((N_REP * CAP,)), dma((3,))],
-        compiler_params=pltpu.CompilerParams(vmem_limit_bytes=VMEM_GRANT),
-    )(back, gate_z, norm_gain.reshape(1, T), got_states, got_tails)
+    mixer, states, tails = finish_call(back, gate_z, norm_gain.reshape(1, T), got_states, got_tails)
     tails = jnp.transpose(tails, (1, 0, 2))[None, :, :, None, :]
     return mixer, states, tails
 

time: 73.4 us -> 69 us (0.940); the launches traced: 72.3 us -> 68.8 us
  Pallas kernels: 71.6 us -> 68.2 us
    pallas_call x1, Pallas kernels: 66 us -> 62.6 us  [body(): pl.pallas_call(main_kernel, name='main', out_shape=[jax.ShapeDtypeStruct(...]
where the time goes in v3:
time: 69 us; the launch traced here: 68.8 us
  Pallas kernels  68.2 us (99%)
    pallas_call x1, Pallas kernels, body(): pl.pallas_call(main_kernel, name='main', out_shape=[jax.ShapeDtypeStruct(...  62.6 us
    pallas_call x1, Pallas kernels, finish_call(): pl.pallas_call(finish_kernel, name='finish', out_shape=[jax.ShapeDtypeStr...  5.63 us

profile of v3, /device:TPU:0, one launch (start us, length us, event | category | flops | bytes accessed | tf_op | source)
XLA Modules:
  0.0 68.8 jit_solution(11723932393510309150)
XLA Ops:
  0.6 62.6 %main.1 = (bf16[16,256,128]{2,1,0:T(8,128)(2,1)}, bf16[8,2,2,128,128]{4,3,2,1,0:T(8,128)(2,1)}, bf16[8,16,512]{2,1,0:T(8,128)(2,1)}) custom-call(bf16[1,16,512,128]{3,2,1,0:T(8,128)(2,1)} %mixed.1, bf16[1,16,2,128]{3,2,1,0:T(2,128)(2,1)} %decay_in.1, bf16[1,16,2,128]{3,2,1,0:T(2,128)(2,1)} %beta_in.1, bf16[1,4,512]{2,1,0:T(4,128)(2,1)} %bitcast.7, f32[2]{0:T(128)} %a_log.1, ...), custom_call_target="tpu_custom_call" | custom-call | tf_op jit(solution)/shard_map/main/pallas_call | solution.py:527
  63.2 5.6 %finish.1 = (bf16[1,16,256,128]{3,2,1,0:T(8,128)(2,1)}, f32[1,16,2,128,128]{4,3,2,1,0:T(8,128)}, bf16[3,16,512]{2,1,0:T(8,128)(2,1)}) custom-call(bf16[16,256,128]{2,1,0:T(8,128)(2,1)} %get-tuple-element.9.back_hbm, bf16[1,16,256,128]{3,2,1,0:T(8,128)(2,1)} %gate.1, f32[1,128]{1,0:T(1,128)} %bitcast.8, ...), custom_call_target="tpu_custom_call" | custom-call | tf_op jit(solution)/shard_map/finish/pallas_call | solution.py:502

commit v4 on v3

--- a/solution.py
+++ b/solution.py
@@ -245,9 +245,9 @@
     return jnp.where(iota((8, 512), 0) == 3, count, rows)
 
 
-ORDER = (1, 15, 4, 12, 5, 11, 3, 13, 2, 14, 6, 10, 8, 7, 9)
+ORDER = (1, 15, 4, 12, 5, 11, 3, 13, 2, 14, 8, 6, 10, 7, 9)
 GROUPS = ((1, 0, 5, 12), (4, 13, 2, 15), (3, 14, 6, 11), (7, 10, 8, 9))
-READY = (0, 6, 10, 12, 15)
+READY = (0, 6, 10, 13, 15)
 REP_ORDER = (2, 6, 1, 7, 3, 5, 4, 0)
 
 
@@ -421,15 +421,18 @@
         pltpu.make_async_copy(got_states_hbm, got_states, load_sem.at[1]),
         pltpu.make_async_copy(gain_hbm, gain, load_sem.at[2])]
 
-    def load(h):
+    def some(g):
+        return pl.ds(4 * g, 4)
+
+    def load(g):
         return [
-            pltpu.make_async_copy(gate.at[0, h], z_in.at[h], gate_sem.at[h]),
-            pltpu.make_async_copy(back_hbm.at[h], back.at[h], back_sem.at[h])]
+            pltpu.make_async_copy(gate.at[0, some(g)], z_in.at[some(g)], gate_sem.at[g]),
+            pltpu.make_async_copy(back_hbm.at[some(g)], back.at[some(g)], back_sem.at[g])]
 
     for copy in first:
         copy.start()
-    for h in range(N_SEQ):
-        for copy in load(h):
+    for g in range(4):
+        for copy in load(g):
             copy.start()
     for copy in first:
         copy.wait()
@@ -439,11 +442,11 @@
         bases.append(base)
         base = base + counts[q]
 
-    def store_states(slot):
-        return pltpu.make_async_copy(states_out.at[slot], states.at[0, slot], states_sem.at[slot])
-
-    def store_mixer(h):
-        return pltpu.make_async_copy(mixed_out.at[h], mixer.at[0, h], mixer_sem.at[h])
+    def store_states(g):
+        return pltpu.make_async_copy(states_out.at[some(g)], states.at[0, some(g)], states_sem.at[g])
+
+    def store_mixer(g):
+        return pltpu.make_async_copy(mixed_out.at[some(g)], mixer.at[0, some(g)], mixer_sem.at[g])
 
     def land(slot):
         pick, used = jnp.int32(0), jnp.int32(0)
@@ -456,7 +459,6 @@
         source, rank = pick // CAP, pick % CAP
         for r in range(2):
             states_out[slot, r] = got_states[source, rank, r].astype(f32) * scale
-        store_states(slot).start()
         both = got_tails[source].astype(f32)
         rows = jnp.where(rank == 0, both[0:8], both[8:16]) * scale
         for p in range(3):
@@ -465,6 +467,7 @@
     def land_some(g, carry):
         for t in range(4):
             land(g * 4 + t)
+        store_states(g).start()
         return carry
 
     lax.fori_loop(0, N_REP * CAP // 4, land_some, 0)
@@ -472,9 +475,8 @@
     column = jnp.broadcast_to(gain[...], (T, T)).T
 
     def norm(g, carry):
-        for t in range(4):
-            for copy in load(g * 4 + t):
-                copy.wait()
+        for copy in load(g):
+            copy.wait()
         for t in range(4):
             h = g * 4 + t
             for r in range(2):
@@ -483,8 +485,7 @@
                 inverse = lax.rsqrt(jnp.mean(value * value, axis=0, keepdims=True) + 1e-6)
                 z = z_in[h, rows, :].astype(f32)
                 mixed_out[h, rows, :] = (value * inverse * column * (z / (1.0 + jnp.exp(-z)))).astype(bf16)
-        for t in range(4):
-            store_mixer(g * 4 + t).start()
+        store_mixer(g).start()
         return carry
 
     lax.fori_loop(0, N_SEQ // 4, norm, 0)
@@ -494,7 +495,7 @@
         store_mixer(h).wait()
         return carry
 
-    lax.fori_loop(0, N_SEQ, drain, 0)
+    lax.fori_loop(0, 4, drain, 0)
 
 
 def finish_call(*operands):
@@ -517,7 +518,7 @@
             pltpu.VMEM((N_REP, CAP, 2, T, T), bf16),
             pltpu.VMEM((N_REP, 16, 512), bf16),
             pltpu.VMEM((3, N_REP * CAP, 512), f32),
-            dma((N_SEQ,)), dma((N_SEQ,)), dma((N_SEQ,)), dma((N_REP * CAP,)), dma((3,))],
+            dma((4,)), dma((4,)), dma((4,)), dma((4,)), dma((3,))],
         compiler_params=pltpu.CompilerParams(vmem_limit_bytes=VMEM_GRANT),
     )(*operands)
 

time: 69 us -> 66.4 us (0.962); the launches traced: 68.8 us -> 65.3 us
  Pallas kernels: 68.2 us -> 64.6 us
    pallas_call x1, Pallas kernels: 62.6 us -> 59.8 us  [body(): pl.pallas_call(main_kernel, name='main', out_shape=[jax.ShapeDtypeStruct(...]
    pallas_call x1, Pallas kernels: 5.63 us -> 4.79 us  [finish_call(): pl.pallas_call(finish_kernel, name='finish', out_shape=[jax.ShapeDtypeStr...]
where the time goes in v4:
time: 66.4 us; the launch traced here: 65.3 us
  Pallas kernels  64.6 us (97%)
    pallas_call x1, Pallas kernels, body(): pl.pallas_call(main_kernel, name='main', out_shape=[jax.ShapeDtypeStruct(...  59.8 us
    pallas_call x1, Pallas kernels, finish_call(): pl.pallas_call(finish_kernel, name='finish', out_shape=[jax.ShapeDtypeStr...  4.79 us

profile of v4, /device:TPU:0, one launch (start us, length us, event | category | flops | bytes accessed | tf_op | source)
XLA Modules:
  0.0 65.3 jit_solution(15562224972863859017)
XLA Ops:
  0.6 59.8 %main.1 = (bf16[16,256,128]{2,1,0:T(8,128)(2,1)}, bf16[8,2,2,128,128]{4,3,2,1,0:T(8,128)(2,1)}, bf16[8,16,512]{2,1,0:T(8,128)(2,1)}) custom-call(bf16[1,16,512,128]{3,2,1,0:T(8,128)(2,1)} %mixed.1, bf16[1,16,2,128]{3,2,1,0:T(2,128)(2,1)} %decay_in.1, bf16[1,16,2,128]{3,2,1,0:T(2,128)(2,1)} %beta_in.1, bf16[1,4,512]{2,1,0:T(4,128)(2,1)} %bitcast.7, f32[2]{0:T(128)} %a_log.1, ...), custom_call_target="tpu_custom_call" | custom-call | tf_op jit(solution)/shard_map/main/pallas_call | solution.py:528
  60.5 4.8 %finish.1 = (bf16[1,16,256,128]{3,2,1,0:T(8,128)(2,1)}, f32[1,16,2,128,128]{4,3,2,1,0:T(8,128)}, bf16[3,16,512]{2,1,0:T(8,128)(2,1)}) custom-call(bf16[16,256,128]{2,1,0:T(8,128)(2,1)} %get-tuple-element.9.back_hbm, bf16[1,16,256,128]{3,2,1,0:T(8,128)(2,1)} %gate.1, f32[1,128]{1,0:T(1,128)} %bitcast.8, ...), custom_call_target="tpu_custom_call" | custom-call | tf_op jit(solution)/shard_map/finish/pallas_call | solution.py:503

commit v5 on v4

--- a/solution.py
+++ b/solution.py
@@ -204,7 +204,7 @@
 
 N_SEQ, N_REP, REQS, CAP = 16, 8, 8, 2
 AHEAD = 11
-BEFORE = 4
+BEFORE = 2
 FIRST = False
 VMEM_GRANT = 63 << 20
 MESH = pl.DeviceIdType.MESH

time: 66.4 us -> 68.8 us (1.036)
  the two profiles are of different devices: /device:TPU:0 before, /device:TPU:2 now
where the time goes in v5:
time: 68.8 us; the launch traced here: 68.7 us
  Pallas kernels  68 us (99%)
    pallas_call x1, Pallas kernels, body(): pl.pallas_call(main_kernel, name='main', out_shape=[jax.ShapeDtypeStruct(...  63.2 us
    pallas_call x1, Pallas kernels, finish_call(): pl.pallas_call(finish_kernel, name='finish', out_shape=[jax.ShapeDtypeStr...  4.79 us

profile of v5, /device:TPU:2, one launch (start us, length us, event | category | flops | bytes accessed | tf_op | source)
XLA Modules:
  0.0 68.7 jit_solution(1242996791807835560)
XLA Ops:
  0.6 63.2 %main.1 = (bf16[16,256,128]{2,1,0:T(8,128)(2,1)}, bf16[8,2,2,128,128]{4,3,2,1,0:T(8,128)(2,1)}, bf16[8,16,512]{2,1,0:T(8,128)(2,1)}) custom-call(bf16[1,16,512,128]{3,2,1,0:T(8,128)(2,1)} %mixed.1, bf16[1,16,2,128]{3,2,1,0:T(2,128)(2,1)} %decay_in.1, bf16[1,16,2,128]{3,2,1,0:T(2,128)(2,1)} %beta_in.1, bf16[1,4,512]{2,1,0:T(4,128)(2,1)} %bitcast.7, f32[2]{0:T(128)} %a_log.1, ...), custom_call_target="tpu_custom_call" | custom-call | tf_op jit(solution)/shard_map/main/pallas_call | solution.py:528
  63.9 4.8 %finish.1 = (bf16[1,16,256,128]{3,2,1,0:T(8,128)(2,1)}, f32[1,16,2,128,128]{4,3,2,1,0:T(8,128)}, bf16[3,16,512]{2,1,0:T(8,128)(2,1)}) custom-call(bf16[16,256,128]{2,1,0:T(8,128)(2,1)} %get-tuple-element.9.back_hbm, bf16[1,16,256,128]{3,2,1,0:T(8,128)(2,1)} %gate.1, f32[1,128]{1,0:T(1,128)} %bitcast.8, ...), custom_call_target="tpu_custom_call" | custom-call | tf_op jit(solution)/shard_map/finish/pallas_call | solution.py:503
